TPU v7x, 32 devices: a whole 2x2x4 slice. The times are simulated.
32 devices in a mesh: dp: 16 (over z, y, x), tensor: 2 (over core).
Axes of the slice: x: 2, y: 2, z: 4, core: 2. Of those that a mesh axis runs over, the one named last changes fastest.
Arguments:
- grads: bfloat16 [16, 256, 3584], P('dp', None, 'tensor'), may hold values from -6 to 6
- residual: float32 [16, 256, 3584], P('dp', None, 'tensor'), may hold values from -4 to 4
- q_prev: float32 [3584, 64], P('tensor'), may hold values from -6 to 6
Outputs:
- q_next: float32 [3584, 64], P('tensor')
- basis: float32 [256, 64], replicated
- new_residual: float32 [16, 256, 3584], P('dp', None, 'tensor')
All inputs are finite; a program needn't handle non-finite values.
Results may differ from a plain program's by a relative error of at most 0.0003.
Values sent between devices are 32-bit elements; how exact they have to be, the bound alone decides.
A program may use at most 64 MiB of HBM per device.

v0:
```python
import jax
import jax.numpy as jnp
from jax import lax
from jax.sharding import PartitionSpec as P


def local(grads, residual, q_prev):
    high = lax.Precision.HIGHEST
    count = lax.axis_size("dp")
    merged = grads[0].astype(jnp.float32) + residual[0]
    partial_left = jnp.dot(merged, q_prev, precision=high)
    left = lax.psum(partial_left, ("dp", "tensor")) / count
    gram = jnp.dot(left.T, left, precision=high)
    lower = jnp.linalg.cholesky(gram)
    basis = jax.scipy.linalg.solve_triangular(lower, left.T, lower=True).T
    q_next = lax.psum(jnp.dot(merged.T, basis, precision=high), "dp") / count
    update = jnp.dot(basis, q_next.T, precision=high)
    new_residual = merged - update
    return (q_next, basis, new_residual[None])


def solution(mesh):
    in_specs = (P("dp", None, "tensor"), P("dp", None, "tensor"), P("tensor", None))
    out_specs = (P("tensor", None), P(), P("dp", None, "tensor"))
    return jax.shard_map(local, mesh=mesh, in_specs=in_specs, out_specs=out_specs, check_vma=False)
```

profile of v0, /device:TPU:0, one launch (start us, length us, event | category | flops | bytes accessed | tf_op | source)
XLA Modules:
  0.0 274.1 jit_solution(10268975559233325000)
XLA Ops:
  7.2 0.0 copy-start
  7.2 0.0 all-reduce.3.cloned.1.call-start
  7.2 0.9 copy-done
  8.2 4.2 %fusion.3 = f32[256,64]{0,1:T(8,128)} fusion(f32[1792,64]{0,1:T(8,128)S(1)} %copy-done, f32[1,256,1792]{2,1,0:T(8,128)} %param.4, bf16[1,256,1792]{2,1,0:T(8,128)(2,1)} %param.3), kind=kOutput, calls=%fused_computation.4 | convolution fusion | flops 353239040 | bytes 3276800 | tf_op jit(solution)/shard_map/dot_general | solution.py:11
  12.4 0.0 all-reduce.3.cloned.1.call-update
  12.4 0.0 all-reduce.5.cloned.1.call-start
  12.4 123.9 %all-reduce.3.cloned.1.call-done = f32[256,64]{0,1:T(8,128)} async-done(((f32[256,64]{0,1:T(8,128)}), f32[256,64]{0,1:T(8,128)}) %all-reduce.3.cloned.1.call-update) | async-done | bytes 65552 | tf_op jit(solution)/shard_map/psum | solution.py:12
  136.3 1.1 fusion.7
  137.4 0.1 copy.6
  137.5 5.8 %cholesky.16 = f32[64,64]{1,0:T(8,128)S(1)} custom-call(f32[64,64]{1,0:T(8,128)S(1)} %fusion.11), custom_call_target="Cholesky" | custom-call | tf_op jit(solution)/shard_map/jit(cholesky)/cholesky | solution.py:14
  143.4 0.6 compare_reduce_fusion
  144.0 0.7 fusion.9
  144.7 4.9 %custom-call.7 = f32[1,64,64]{1,2,0:T(8,128)S(1)} custom-call(f32[1,64,64]{2,1,0:T(8,128)S(1)} %fusion.9), custom_call_target="InvertDiagBlocksLowerTriangular" | custom-call | tf_op jit(solution)/shard_map/jit(_solve_triangular)/triangular_solve | solution.py:15
  149.6 1.1 fusion.5
  150.7 0.0 copy-done.1
  150.7 0.0 copy-done.2
  150.7 0.0 copy-start.4
  150.7 2.2 fusion.1
  152.9 0.0 all-reduce.5.cloned.1.call-update
  152.9 110.3 %all-reduce.5.cloned.1.call-done = f32[1792,64]{0,1:T(8,128)} async-done(((f32[1792,64]{0,1:T(8,128)}), f32[1792,64]{0,1:T(8,128)}) %all-reduce.5.cloned.1.call-update) | async-done | bytes 458768 | tf_op jit(solution)/shard_map/psum | solution.py:16
  263.3 1.0 broadcast_multiply_fusion
  264.3 0.0 copy-start.3
  264.3 2.9 %fusion = f32[1,256,1792]{2,1,0:T(8,128)} fusion(f32[64,256]{1,0:T(8,128)S(1)} %fusion.5, f32[1792,64]{0,1:T(8,128)S(1)} %broadcast_multiply_fusion, f32[1,256,1792]{2,1,0:T(8,128)S(1)} %copy-done.1, bf16[1,256,1792]{2,1,0:T(8,128)(2,1)S(1)} %copy-done.2), kind=kOutput, calls=%fused_computation.1 | convolution fusion | flops 353697792 | bytes 5111808 | tf_op jit(solution)/shard_map/dot_general | solution.py:17
  267.2 0.0 copy-done.3
  (5 shorter events, 0.0 us)
Async XLA Ops:
  7.2 1.0 copy-start
  7.2 143.5 %copy-start.1 = (f32[1,256,1792]{2,1,0:T(8,128)S(1)}, f32[1,256,1792]{2,1,0:T(8,128)}, u32[]{:S(2)}) copy-start(f32[1,256,1792]{2,1,0:T(8,128)} %param.4) | copy-start | bytes 5505028
  7.2 143.5 %copy-start.2 = (bf16[1,256,1792]{2,1,0:T(8,128)(2,1)S(1)}, bf16[1,256,1792]{2,1,0:T(8,128)(2,1)}, u32[]{:S(2)}) copy-start(bf16[1,256,1792]{2,1,0:T(8,128)(2,1)} %param.3) | copy-start | bytes 2752516
  7.2 129.1 %all-reduce.3.cloned.1.call-start = ((), (), s32[]{:S(2)}) async-start(), calls=%async_computation | async-start | bytes 131072 | tf_op jit(solution)/shard_map/psum | solution.py:12
  12.4 250.9 %all-reduce.5.cloned.1.call-start = ((), (), s32[]{:S(2)}) async-start(), calls=%async_computation.1 | async-start | bytes 917504 | tf_op jit(solution)/shard_map/psum | solution.py:16
  150.7 113.6 %copy-start.4 = (f32[64,256]{1,0:T(8,128)}, f32[64,256]{1,0:T(8,128)S(1)}, u32[]{:S(2)}) copy-start(f32[64,256]{1,0:T(8,128)S(1)} %fusion.5) | copy-start | bytes 196612
  264.3 2.9 %copy-start.3 = (f32[1792,64]{0,1:T(8,128)}, f32[1792,64]{0,1:T(8,128)S(1)}, u32[]{:S(2)}) copy-start(f32[1792,64]{0,1:T(8,128)S(1)} %broadcast_multiply_fusion) | copy-start | bytes 1376260
Sparse Core Ops, SparseCore 0:
  14.2 122.1 all-reduce.2
  153.1 110.1 all-reduce.4
where the time goes:
time: 274 us
  waiting for transfers between devices  234 us (85%)
  between operations  14.1 us (5%)
  other arithmetic  13.1 us (5%)
  matrix products  11.4 us (4%)
    psum x1, waiting for transfers between devices, local(): left = lax.psum(partial_left, ('dp', 'tensor')) / count  124 us
    psum x1, waiting for transfers between devices, local(): q_next = lax.psum(jnp.dot(merged.T, basis, precision=high), 'dp') / count  110 us
    another operation x3, other arithmetic, local(): lower = jnp.linalg.cholesky(gram)  6.52 us
    another operation x2, other arithmetic, local(): basis = jax.scipy.linalg.solve_triangular(lower, left.T, lower=True).T  5.55 us
  transfers between devices with their start and end apart: 2, of which 2 were waited for; matrix products, arithmetic and copies ran while one was open for 0% of the time, Pallas kernels for 0%

commit v1 on v0

v1 whole, which is shorter than its diff:
```python
import functools

import jax
import jax.numpy as jnp
from jax import lax
from jax.experimental import pallas as pl
from jax.experimental.pallas import tpu as pltpu
from jax.sharding import PartitionSpec as P

MESH = pl.DeviceIdType.MESH
HIGHEST = lax.Precision.HIGHEST
SUB, LANE = 8, 128


def split(x):
    hi = x.astype(jnp.bfloat16)
    lo = (x - hi.astype(jnp.float32)).astype(jnp.bfloat16)
    return hi, lo


def dot(a, b, dims=((1,), (0,)), precision=None):
    return lax.dot_general(a, b, (dims, ((), ())), precision=precision, preferred_element_type=jnp.float32)


def eliminate(tiles, start, stop, rank):
    tiles = list(tiles)
    index = lax.broadcasted_iota(jnp.int32, tiles[0].shape, 0)
    for k in range(start, stop):
        block, r = divmod(k, SUB)
        row = tiles[block][r : r + 1, :]
        scaled = row * (1.0 / row[:, k : k + 1])
        for b in range(block, rank // SUB):
            if b == block and r == SUB - 1:
                continue
            column = tiles[b][:, k : k + 1]
            if b == block:
                column = jnp.where(index[:, :1] > r, column, 0.0)
            tiles[b] = tiles[b] - column * scaled
    return tiles


def kernel(
    n, inner, outer, tensor,
    g_ref, r_ref, q_ref, new_ref, next_ref, basis_ref,
    m_hi, m_lo, left_own, left_in, left_mid, left_all,
    t_own, t_in, t_sum, t_in2, t_all, gram_b, sems_send, sems_recv,
):
    rows, cols = g_ref.shape
    rank = q_ref.shape[0]
    block = 2 * LANE
    me_dp, me_t = lax.axis_index("dp"), lax.axis_index("tensor")
    i, o = lax.rem(me_dp, inner), lax.div(me_dp, inner)
    near = inner * tensor
    place = i * tensor + me_t

    def near_device(k):
        peer = lax.rem(place + k, near)
        return peer, (o * inner + lax.div(peer, tensor), lax.rem(peer, tensor))

    def plane_device(k):
        peer = lax.rem(i + k, inner)
        return peer, (o * inner + peer, me_t)

    def far_device(k):
        peer = lax.rem(o + k, outer)
        return peer, (peer * inner + i, me_t)

    barrier = pltpu.get_barrier_semaphore()
    for k in range(1, near):
        pl.semaphore_signal(barrier, inc=1, device_id=near_device(k)[1], device_id_type=MESH)
    for k in range(1, outer):
        pl.semaphore_signal(barrier, inc=1, device_id=far_device(k)[1], device_id_type=MESH)

    used = [0]

    def send(src, dst, device):
        slot = used[0]
        used[0] += 1
        copy = pltpu.make_async_remote_copy(
            src_ref=src, dst_ref=dst, send_sem=sems_send.at[slot], recv_sem=sems_recv.at[slot],
            device_id=device, device_id_type=MESH,
        )
        copy.start()
        return copy

    sent = []

    def arrive(copies):
        for copy in copies:
            copy.wait_recv()
        sent.extend(copies)

    q_hi, q_lo = split(q_ref[...])
    q_two = jnp.concatenate([q_hi, q_lo], axis=0)
    total = jnp.zeros((2 * rank, rows), jnp.float32)
    low = jnp.zeros((rank, rows), jnp.float32)
    for c in range(0, cols, block):
        hi, lo = split(g_ref[:, c : c + block].astype(jnp.float32) + r_ref[:, c : c + block])
        m_hi[:, c : c + block] = hi
        m_lo[:, c : c + block] = lo
        total += dot(q_two[:, c : c + block], hi, ((1,), (1,)))
        low += dot(q_hi[:, c : c + block], lo, ((1,), (1,)))
    part = (total[:rank] + total[rank:]) + low
    tall = rank // SUB
    left_tiles = tall * (rows // LANE)
    for b in range(rows // LANE):
        left_own[b * tall : (b + 1) * tall] = part[:, b * LANE : (b + 1) * LANE].reshape(tall, SUB, LANE)
    if left_own.shape[0] > left_tiles:
        left_own[left_tiles:] = jnp.zeros((left_own.shape[0] - left_tiles, SUB, LANE), jnp.float32)
    piece = left_own.shape[0] // near

    pl.semaphore_wait(barrier, near - 1 + outer - 1)

    copies = []
    for k in range(1, near):
        peer, device = near_device(k)
        copies.append(send(left_own.at[pl.ds(peer * piece, piece)], left_in.at[k], device))
    arrive(copies)
    value = left_own[pl.ds(place * piece, piece)]
    for k in range(1, near):
        value += left_in[k]
    left_mid[o] = value
    copies = []
    for k in range(1, outer):
        _, device = far_device(k)
        copies.append(send(left_mid.at[o], left_mid.at[o], device))
    arrive(copies)
    value = left_mid[0]
    for k in range(1, outer):
        value += left_mid[k]
    here = left_all.at[pl.ds(place * piece, piece)]
    here[...] = value / n
    copies = []
    for k in range(1, near):
        copies.append(send(here, here, near_device(k)[1]))
    arrive(copies)
    left = jnp.concatenate(
        [left_all[b * tall : (b + 1) * tall].reshape(rank, LANE) for b in range(rows // LANE)], axis=1
    )

    l_hi, l_lo = split(left)
    l_two = jnp.concatenate([l_hi, l_lo], axis=0)
    t_tiles = tall * (cols // LANE)
    for c in range(0, cols, block):
        both = dot(l_two, m_hi[:, c : c + block])
        value = (both[:rank] + both[rank:]) + dot(l_hi, m_lo[:, c : c + block])
        for d in range(0, block, LANE):
            b = (c + d) // LANE
            t_own[b * tall : (b + 1) * tall] = value[:, d : d + LANE].reshape(tall, SUB, LANE)
    if t_own.shape[0] > t_tiles:
        t_own[t_tiles:] = jnp.zeros((t_own.shape[0] - t_tiles, SUB, LANE), jnp.float32)
    small = t_own.shape[0] // n
    large = small * outer

    copies = []
    for k in range(1, inner):
        peer, device = plane_device(k)
        copies.append(send(t_own.at[pl.ds(peer * large, large)], t_in.at[k], device))

    gram_b[:rank] = left
    gram_b[rank:] = jnp.zeros_like(left)
    gram = dot(left, gram_b[...], ((1,), (1,)), HIGHEST)
    row_id = lax.broadcasted_iota(jnp.int32, gram.shape, 0)
    lane_id = lax.broadcasted_iota(jnp.int32, gram.shape, 1)
    gram = gram + jnp.where(lane_id == row_id + rank, 1.0, 0.0)
    tiles = [gram[b : b + SUB] for b in range(0, rank, SUB)]
    tiles = eliminate(tiles, 0, rank, rank)
    done = jnp.concatenate(tiles, axis=0)
    pivot = jnp.sum(jnp.where(lane_id == row_id, done, 0.0), axis=1, keepdims=True)
    done = done * (1.0 / jnp.sqrt(pivot))
    w_two = jnp.where(lane_id < rank, pltpu.roll(done, rank, 1), done)
    basis = dot(w_two[:, :rank], left, precision=HIGHEST)
    basis_ref[...] = basis
    b_hi, b_lo = split(jnp.concatenate([basis, basis], axis=0).T)
    b_four = jnp.concatenate([b_hi, b_lo], axis=1)
    w_hi, w_lo = split(w_two / n)
    w_four = jnp.concatenate([w_hi, w_lo], axis=1)

    arrive(copies)
    mine = t_own[pl.ds(i * large, large)]
    for k in range(1, inner):
        mine += t_in[k]
    t_sum[...] = mine
    copies = []
    for k in range(1, outer):
        peer, device = far_device(k)
        copies.append(send(t_sum.at[pl.ds(peer * small, small)], t_in2.at[k], device))
    arrive(copies)
    mine = t_sum[pl.ds(o * small, small)]
    for k in range(1, outer):
        mine += t_in2[k]
    here = t_all.at[pl.ds(i * large + o * small, small)]
    here[...] = mine
    copies = []
    for k in range(1, outer):
        copies.append(send(here, here, far_device(k)[1]))
    arrive(copies)
    here = t_all.at[pl.ds(i * large, large)]
    copies = []
    for k in range(1, inner):
        copies.append(send(here, here, plane_device(k)[1]))
    arrive(copies)

    for c in range(0, cols, block):
        t = jnp.concatenate(
            [t_all[b * tall : (b + 1) * tall].reshape(rank, LANE) for b in range(c // LANE, (c + block) // LANE)],
            axis=1,
        )
        t_hi, t_lo = split(t)
        q_next = dot(w_four, jnp.concatenate([t_hi, t_lo, t_hi, t_lo], axis=0))
        next_ref[:, c : c + block] = q_next
        n_hi, n_lo = split(q_next)
        update = dot(b_four, jnp.concatenate([n_hi, n_lo, n_hi, n_lo], axis=0))
        merged = g_ref[:, c : c + block].astype(jnp.float32) + r_ref[:, c : c + block]
        new_ref[:, c : c + block] = merged - update

    for copy in sent:
        copy.wait_send()


def local(grads, residual, q_prev):
    n, tensor = lax.axis_size("dp"), lax.axis_size("tensor")
    inner = max(d for d in range(1, n + 1) if n % d == 0 and d * d <= n)
    outer = n // inner
    rows, cols = grads.shape[1:]
    rank = q_prev.shape[1]
    near = inner * tensor
    left_piece = pl.cdiv((rank // SUB) * (rows // LANE), near)
    small = pl.cdiv((rank // SUB) * (cols // LANE), n)
    copies = 2 * (near - 1) + 3 * (outer - 1) + 2 * (inner - 1)
    f32 = jnp.float32
    tile = lambda *dims: pltpu.VMEM((*dims, SUB, LANE), f32)
    vmem = pl.BlockSpec(memory_space=pltpu.VMEM)
    new, q_next, basis = pl.pallas_call(
        functools.partial(kernel, n, inner, outer, tensor),
        out_shape=(
            jax.ShapeDtypeStruct((rows, cols), f32),
            jax.ShapeDtypeStruct((rank, cols), f32),
            jax.ShapeDtypeStruct((rank, rows), f32),
        ),
        in_specs=[vmem] * 3,
        out_specs=(vmem,) * 3,
        scratch_shapes=[
            pltpu.VMEM((rows, cols), jnp.bfloat16),
            pltpu.VMEM((rows, cols), jnp.bfloat16),
            tile(near * left_piece),
            tile(near, left_piece),
            tile(outer, left_piece),
            tile(near * left_piece),
            tile(n * small),
            tile(inner, outer * small),
            tile(outer * small),
            tile(outer, small),
            tile(n * small),
            pltpu.VMEM((2 * rank, rows), f32),
            pltpu.SemaphoreType.DMA((copies,)),
            pltpu.SemaphoreType.DMA((copies,)),
        ],
        compiler_params=pltpu.CompilerParams(collective_id=0, has_side_effects=True),
        name="powersgd",
    )(grads[0], residual[0], q_prev.T)
    return (q_next.T, basis.T, new[None])


def solution(mesh):
    in_specs = (P("dp", None, "tensor"), P("dp", None, "tensor"), P("tensor", None))
    out_specs = (P("tensor", None), P(), P("dp", None, "tensor"))
    return jax.shard_map(local, mesh=mesh, in_specs=in_specs, out_specs=out_specs, check_vma=False)
```

time: 274 us -> 54.1 us (0.20)
  waiting for transfers between devices: 234 us -> 0 us
  Pallas kernels: 0 us -> 47.1 us
  between operations: 14.1 us -> 0.64 us
  other arithmetic: 13.1 us -> 0 us
  matrix products: 11.4 us -> 0 us
  local copies, waits for them, and re-layouts: 1.05 us -> 6.13 us
    psum x2 -> x0, waiting for transfers between devices: 234 us -> none  [the longest x1 124 us: local(): left = lax.psum(partial_left, ('dp', 'tensor')) / count]
    pallas_call x0 -> x1, Pallas kernels: none -> 47.1 us  [local(): pl.pallas_call(functools.partial(kernel, n, inner, outer, tensor), out_sh...]
    another operation x5 -> x0, other arithmetic: 12.1 us -> none  [the longest x3 6.52 us: local(): lower = jnp.linalg.cholesky(gram)]
    dot_general x4 -> x0, matrix products: 10.3 us -> none  [the longest x1 4.17 us: local(): partial_left = jnp.dot(merged, q_prev, precision=high)]
    unnamed x10 -> x3, local copies, waits for them, and re-layouts: 0.97 us -> 6.13 us
  transfers between devices with their start and end apart: 2 -> 0, of which waited for: 2 -> 0; matrix products, arithmetic and copies ran while one was open for 0% -> 0% of each run, Pallas kernels for 0% -> 0%
where the time goes in v1:
time: 54.1 us; the launch traced here: 53.9 us
  Pallas kernels  47.1 us (87%)
  local copies, waits for them, and re-layouts  6.13 us (11%)
  between operations  0.64 us (1%)
    pallas_call x1, Pallas kernels, local(): pl.pallas_call(functools.partial(kernel, n, inner, outer, tensor), out_sh...  47.1 us
    unnamed x3, local copies, waits for them, and re-layouts  6.13 us

profile of v1, /device:TPU:0, one launch (start us, length us, event | category | flops | bytes accessed | tf_op | source)
XLA Modules:
  0.0 53.9 jit_solution(8826804444125899182)
XLA Ops:
  0.6 47.1 %powersgd.1 = (f32[256,1792]{1,0:T(8,128)}, f32[64,1792]{1,0:T(8,128)}, f32[64,256]{1,0:T(8,128)}) custom-call(bf16[256,1792]{1,0:T(8,128)(2,1)} %bitcast.8, f32[256,1792]{1,0:T(8,128)} %bitcast.6, f32[64,1792]{1,0:T(8,128)} %bitcast.9), custom_call_target="tpu_custom_call" | custom-call | tf_op jit(solution)/shard_map/powersgd/pallas_call | solution.py:234
  47.7 1.8 %copy.9 = f32[1792,64]{0,1:T(8,128)} copy(f32[1792,64]{0,1:T(8,128)} %bitcast.10) | data formatting | bytes 917504
  49.6 1.5 %copy.10 = f32[256,64]{0,1:T(8,128)} copy(f32[256,64]{0,1:T(8,128)} %bitcast.11) | data formatting | bytes 131072
  51.0 2.8 %copy.11 = f32[1,256,1792]{2,1,0:T(8,128)} copy(f32[1,256,1792]{2,1,0:T(8,128)} %bitcast.7) | data formatting | bytes 3670016

commit v2 on v1

v2 whole, which is shorter than its diff:
```python
import functools

import jax
import jax.numpy as jnp
from jax import lax
from jax.experimental import pallas as pl
from jax.experimental.pallas import tpu as pltpu
from jax.sharding import PartitionSpec as P

MESH = pl.DeviceIdType.MESH
HIGHEST = lax.Precision.HIGHEST
SUB, LANE = 8, 128
FIRST_STEPS = 40
VMEM_LIMIT = 24 << 20


def split(x):
    hi = x.astype(jnp.bfloat16)
    lo = (x - hi.astype(jnp.float32)).astype(jnp.bfloat16)
    return hi, lo


def dot(a, b, dims=((1,), (0,)), precision=None):
    return lax.dot_general(a, b, (dims, ((), ())), precision=precision, preferred_element_type=jnp.float32)


def eliminate(tiles, start, stop, rank):
    tiles = list(tiles)
    index = lax.broadcasted_iota(jnp.int32, tiles[0].shape, 0)
    for k in range(start, stop):
        block, r = divmod(k, SUB)
        row = tiles[block][r : r + 1, :]
        scaled = row * (1.0 / row[:, k : k + 1])
        for b in range(block, rank // SUB):
            if b == block and r == SUB - 1:
                continue
            column = tiles[b][:, k : k + 1]
            if b == block:
                column = jnp.where(index[:, :1] > r, column, 0.0)
            tiles[b] = tiles[b] - column * scaled
    return tiles


def reduce_kernel(
    n, inner, outer, tensor,
    g_hbm, r_hbm, q_ref, m_ref, t_ref, b_ref, w_ref, basis_ref,
    g_in, r_in, m_hi, m_lo, left_own, left_in, left_mid, left_all,
    t_own, t_in, t_sum, t_in2, t_all, gram_b, sems_load, sems_send, sems_recv,
):
    rows, cols = g_in.shape
    rank = q_ref.shape[0]
    block = 2 * LANE
    starts = range(0, cols, block)
    loads = []
    for j, c in enumerate(starts):
        here = pl.ds(c, block)
        pair = (
            pltpu.make_async_copy(g_hbm.at[:, here], g_in.at[:, here], sems_load.at[0, j]),
            pltpu.make_async_copy(r_hbm.at[:, here], r_in.at[:, here], sems_load.at[1, j]),
        )
        for copy in pair:
            copy.start()
        loads.append(pair)

    me_dp, me_t = lax.axis_index("dp"), lax.axis_index("tensor")
    i, o = lax.rem(me_dp, inner), lax.div(me_dp, inner)
    near = inner * tensor
    place = i * tensor + me_t

    def near_device(k):
        peer = lax.rem(place + k, near)
        return peer, (o * inner + lax.div(peer, tensor), lax.rem(peer, tensor))

    def plane_device(k):
        peer = lax.rem(i + k, inner)
        return peer, (o * inner + peer, me_t)

    def far(j):
        low = jnp.where(outer - 1 - j > o, outer - 1 - j, outer - 2 - j)
        high = jnp.where(j < o, j, j + 1)
        return jnp.where(2 * o < outer, low, high)

    def far_device(peer):
        return (peer * inner + i, me_t)

    barrier = pltpu.get_barrier_semaphore()
    for k in range(1, near):
        pl.semaphore_signal(barrier, inc=1, device_id=near_device(k)[1], device_id_type=MESH)
    for k in range(1, outer):
        pl.semaphore_signal(barrier, inc=1, device_id=far_device(lax.rem(o + k, outer)), device_id_type=MESH)

    used = [0]
    sent = []

    def slots(count):
        used[0] += count
        return used[0] - count

    def remote(src, dst, slot, device):
        return pltpu.make_async_remote_copy(
            src_ref=src, dst_ref=dst, send_sem=sems_send.at[len(sent)], recv_sem=sems_recv.at[slot],
            device_id=device, device_id_type=MESH,
        )

    def send(src, dst, slot, device):
        copy = remote(src, dst, slot, device)
        copy.start()
        sent.append(copy)
        return copy

    def landed(dst, slot):
        remote(dst, dst, slot, near_device(1)[1]).wait_recv()

    q_hi, q_lo = split(q_ref[...])
    q_two = jnp.concatenate([q_hi, q_lo], axis=0)
    total = jnp.zeros((2 * rank, rows), jnp.float32)
    low = jnp.zeros((rank, rows), jnp.float32)
    for (load_g, load_r), c in zip(loads, starts):
        load_g.wait()
        load_r.wait()
        merged = g_in[:, c : c + block].astype(jnp.float32) + r_in[:, c : c + block]
        m_ref[:, c : c + block] = merged
        hi, lo = split(merged)
        m_hi[:, c : c + block] = hi
        m_lo[:, c : c + block] = lo
        total += dot(q_two[:, c : c + block], hi, ((1,), (1,)))
        low += dot(q_hi[:, c : c + block], lo, ((1,), (1,)))
    part = (total[:rank] + total[rank:]) + low
    tall = rank // SUB
    left_tiles = tall * (rows // LANE)
    for b in range(rows // LANE):
        left_own[b * tall : (b + 1) * tall] = part[:, b * LANE : (b + 1) * LANE].reshape(tall, SUB, LANE)
    if left_own.shape[0] > left_tiles:
        left_own[left_tiles:] = jnp.zeros((left_own.shape[0] - left_tiles, SUB, LANE), jnp.float32)
    piece = left_own.shape[0] // near

    pl.semaphore_wait(barrier, near - 1 + outer - 1)

    base = slots(near)
    copies = []
    for k in range(1, near):
        peer, device = near_device(k)
        copies.append(send(left_own.at[pl.ds(peer * piece, piece)], left_in.at[k], base + k, device))
    value = left_own[pl.ds(place * piece, piece)]
    for k, copy in enumerate(copies):
        copy.wait_recv()
        value += left_in[k + 1]
    left_mid[o] = value
    base = slots(outer)
    for j in range(outer - 1):
        send(left_mid.at[o], left_mid.at[o], base + o, far_device(far(j)))
    for j in reversed(range(outer - 1)):
        landed(left_mid.at[far(j)], base + far(j))
    value = left_mid[0]
    for k in range(1, outer):
        value += left_mid[k]
    here = left_all.at[pl.ds(place * piece, piece)]
    here[...] = value / n
    base = slots(near)
    copies = [send(here, here, base + k, near_device(k)[1]) for k in range(1, near)]
    for copy in copies:
        copy.wait_recv()
    left = jnp.concatenate(
        [left_all[b * tall : (b + 1) * tall].reshape(rank, LANE) for b in range(rows // LANE)], axis=1
    )

    l_hi, l_lo = split(left)
    l_two = jnp.concatenate([l_hi, l_lo], axis=0)
    t_tiles = tall * (cols // LANE)
    for c in starts:
        both = dot(l_two, m_hi[:, c : c + block])
        value = (both[:rank] + both[rank:]) + dot(l_hi, m_lo[:, c : c + block])
        for d in range(0, block, LANE):
            b = (c + d) // LANE
            t_own[b * tall : (b + 1) * tall] = value[:, d : d + LANE].reshape(tall, SUB, LANE)
    if t_own.shape[0] > t_tiles:
        t_own[t_tiles:] = jnp.zeros((t_own.shape[0] - t_tiles, SUB, LANE), jnp.float32)
    small = t_own.shape[0] // n
    large = small * outer

    order = [far(j) for j in range(outer - 1)] + [o]
    base = slots(outer * inner)
    steps = []
    for j, b in enumerate(order):
        copies = []
        for k in range(1, inner):
            peer, device = plane_device(k)
            copies.append(send(
                t_own.at[pl.ds(peer * large + b * small, small)], t_in.at[k, pl.ds(b * small, small)],
                base + j * inner + k, device,
            ))
        steps.append(copies)

    gram_b[:rank] = left
    gram_b[rank:] = jnp.zeros_like(left)
    gram = dot(left, gram_b[...], ((1,), (1,)), HIGHEST)
    row_id = lax.broadcasted_iota(jnp.int32, gram.shape, 0)
    lane_id = lax.broadcasted_iota(jnp.int32, gram.shape, 1)
    gram = gram + jnp.where(lane_id == row_id + rank, 1.0, 0.0)
    tiles = [gram[b : b + SUB] for b in range(0, rank, SUB)]
    middle = FIRST_STEPS * rank // 64
    tiles = eliminate(tiles, 0, middle, rank)

    base = slots(outer)
    for copies, b in zip(steps, order):
        mine = t_own[pl.ds(i * large + b * small, small)]
        for k, copy in enumerate(copies):
            copy.wait_recv()
            mine += t_in[k + 1, pl.ds(b * small, small)]
        there = t_sum.at[pl.ds(b * small, small)]
        there[...] = mine
        if copies is not steps[-1]:
            send(there, t_in2.at[o], base + o, far_device(b))

    tiles = eliminate(tiles, middle, rank, rank)

    mine = t_sum[pl.ds(o * small, small)]
    for b in order[:-1]:
        landed(t_in2.at[b], base + b)
        mine += t_in2[b]
    here = t_all.at[pl.ds(i * large + o * small, small)]
    here[...] = mine
    base = slots(outer)
    for b in order[:-1]:
        send(here, here, base + o, far_device(b))
    last = slots(inner * outer)

    def spread(b):
        part = t_all.at[pl.ds(i * large + b * small, small)]
        for k in range(1, inner):
            send(part, part, last + k * outer + b, plane_device(k)[1])

    spread(o)

    done = jnp.concatenate(tiles, axis=0)
    pivot = jnp.sum(jnp.where(lane_id == row_id, done, 0.0), axis=1, keepdims=True)
    done = done * (1.0 / jnp.sqrt(pivot))
    w_two = jnp.where(lane_id < rank, pltpu.roll(done, rank, 1), done)
    basis = dot(w_two[:, :rank], left, precision=HIGHEST)
    basis_ref[...] = basis
    w_hi, w_lo = split(w_two / n)
    w_ref[...] = jnp.concatenate([w_hi, w_lo], axis=1)

    for b in reversed(order[:-1]):
        landed(t_all.at[pl.ds(i * large + b * small, small)], base + b)
        spread(b)

    b_hi, b_lo = split(jnp.concatenate([basis, basis], axis=0).T)
    b_ref[...] = jnp.concatenate([b_hi, b_lo], axis=1)

    for b in range(outer):
        for k in range(1, inner):
            peer = lax.rem(i + inner - k, inner)
            landed(t_all.at[pl.ds(peer * large + b * small, small)], last + k * outer + b)
    t_ref[...] = t_all[:t_tiles]
    for copy in sent:
        copy.wait_send()


def finish_kernel(
    m_ref, t_ref, b_ref, w_ref, basis_ref, new_hbm, next_hbm, out_basis_ref,
    new_out, next_out, sems_store,
):
    rank, cols = next_out.shape
    tall = rank // SUB
    block = 2 * LANE
    out_basis_ref[...] = basis_ref[...]
    stores = []
    for j, c in enumerate(range(0, cols, block)):
        here = pl.ds(c, block)
        t = jnp.concatenate(
            [t_ref[b * tall : (b + 1) * tall].reshape(rank, LANE) for b in range(c // LANE, (c + block) // LANE)],
            axis=1,
        )
        t_hi, t_lo = split(t)
        q_next = dot(w_ref[...], jnp.concatenate([t_hi, t_lo, t_hi, t_lo], axis=0))
        next_out[:, c : c + block] = q_next
        stores.append(pltpu.make_async_copy(next_out.at[:, here], next_hbm.at[:, here], sems_store.at[0, j]))
        stores[-1].start()
        n_hi, n_lo = split(q_next)
        update = dot(b_ref[...], jnp.concatenate([n_hi, n_lo, n_hi, n_lo], axis=0))
        new_out[:, c : c + block] = m_ref[:, c : c + block] - update
        stores.append(pltpu.make_async_copy(new_out.at[:, here], new_hbm.at[:, here], sems_store.at[1, j]))
        stores[-1].start()
    for copy in stores:
        copy.wait()


def local(grads, residual, q_prev):
    n, tensor = lax.axis_size("dp"), lax.axis_size("tensor")
    inner = max(d for d in range(1, n + 1) if n % d == 0 and d * d <= n)
    outer = n // inner
    rows, cols = grads.shape[1:]
    rank = q_prev.shape[1]
    near = inner * tensor
    t_tiles = (rank // SUB) * (cols // LANE)
    left_piece = pl.cdiv((rank // SUB) * (rows // LANE), near)
    small = pl.cdiv(t_tiles, n)
    copies = 2 * near + 4 * outer + 2 * inner * outer
    f32, bf16 = jnp.float32, jnp.bfloat16
    tile = lambda *dims: pltpu.VMEM((*dims, SUB, LANE), f32)
    vmem = pl.BlockSpec(memory_space=pltpu.VMEM)
    hbm = pl.BlockSpec(memory_space=pltpu.HBM)
    chunks = cols // (2 * LANE)
    merged, t_sum, b_four, w_four, basis = pl.pallas_call(
        functools.partial(reduce_kernel, n, inner, outer, tensor),
        out_shape=(
            jax.ShapeDtypeStruct((rows, cols), f32),
            jax.ShapeDtypeStruct((t_tiles, SUB, LANE), f32),
            jax.ShapeDtypeStruct((rows, 4 * rank), bf16),
            jax.ShapeDtypeStruct((rank, 4 * rank), bf16),
            jax.ShapeDtypeStruct((rank, rows), f32),
        ),
        in_specs=[hbm, hbm, vmem],
        out_specs=(vmem,) * 5,
        scratch_shapes=[
            pltpu.VMEM((rows, cols), bf16),
            pltpu.VMEM((rows, cols), f32),
            pltpu.VMEM((rows, cols), bf16),
            pltpu.VMEM((rows, cols), bf16),
            tile(near * left_piece),
            tile(near, left_piece),
            tile(outer, left_piece),
            tile(near * left_piece),
            tile(n * small),
            tile(inner, outer * small),
            tile(outer * small),
            tile(outer, small),
            tile(n * small),
            pltpu.VMEM((2 * rank, rows), f32),
            pltpu.SemaphoreType.DMA((2, chunks)),
            pltpu.SemaphoreType.DMA((copies,)),
            pltpu.SemaphoreType.DMA((copies,)),
        ],
        compiler_params=pltpu.CompilerParams(collective_id=0, has_side_effects=True, vmem_limit_bytes=VMEM_LIMIT),
        name="reduce",
    )(grads[0], residual[0], q_prev.T)
    new, q_next, basis = pl.pallas_call(
        finish_kernel,
        out_shape=(
            jax.ShapeDtypeStruct((rows, cols), f32),
            jax.ShapeDtypeStruct((rank, cols), f32),
            jax.ShapeDtypeStruct((rank, rows), f32),
        ),
        in_specs=[vmem] * 5,
        out_specs=(hbm, hbm, vmem),
        scratch_shapes=[
            pltpu.VMEM((rows, cols), f32),
            pltpu.VMEM((rank, cols), f32),
            pltpu.SemaphoreType.DMA((2, chunks)),
        ],
        compiler_params=pltpu.CompilerParams(vmem_limit_bytes=VMEM_LIMIT),
        name="finish",
    )(merged, t_sum, b_four, w_four, basis)
    return (q_next.T, basis.T, new[None])


def solution(mesh):
    in_specs = (P("dp", None, "tensor"), P("dp", None, "tensor"), P("tensor", None))
    out_specs = (P("tensor", None), P(), P("dp", None, "tensor"))
    return jax.shard_map(local, mesh=mesh, in_specs=in_specs, out_specs=out_specs, check_vma=False)
```

time: 54.1 us -> 42.3 us (0.78)
  Pallas kernels: 47.1 us -> 37.8 us
  local copies, waits for them, and re-layouts: 6.13 us -> 3.69 us
    pallas_call x1 -> x2, Pallas kernels: 47.1 us -> 37.8 us  [the longest x1 35.2 us: local(): pl.pallas_call(functools.partial(reduce_kernel, n, inner, outer, tensor),...]
    unnamed x3 -> x6, local copies, waits for them, and re-layouts: 6.13 us -> 3.69 us
where the time goes in v2:
time: 42.3 us; the launch traced here: 42.1 us
  Pallas kernels  37.8 us (89%)
  local copies, waits for them, and re-layouts  3.69 us (9%)
  between operations  0.65 us (2%)
    pallas_call x1, Pallas kernels, local(): pl.pallas_call(functools.partial(reduce_kernel, n, inner, outer, tensor),...  35.2 us
    unnamed x6, local copies, waits for them, and re-layouts  3.69 us
    pallas_call x1, Pallas kernels, local(): pl.pallas_call(finish_kernel, out_shape=(jax.ShapeDtypeStruct((rows, cols...  2.58 us

profile of v2, /device:TPU:0, one launch (start us, length us, event | category | flops | bytes accessed | tf_op | source)
XLA Modules:
  0.0 42.1 jit_solution(10310907720182892820)
XLA Ops:
  0.6 0.0 copy-start
  0.6 1.5 %copy-done = f32[1,256,1792]{2,1,0:T(8,128)S(1)} copy-done((f32[1,256,1792]{2,1,0:T(8,128)S(1)}, f32[1,256,1792]{2,1,0:T(8,128)}, u32[]{:S(2)}) %copy-start) | copy-done | bytes 1835032
  2.1 0.0 copy-start.1
  2.1 1.2 %copy-done.1 = bf16[1,256,1792]{2,1,0:T(8,128)(2,1)S(1)} copy-done((bf16[1,256,1792]{2,1,0:T(8,128)(2,1)S(1)}, bf16[1,256,1792]{2,1,0:T(8,128)(2,1)}, u32[]{:S(2)}) %copy-start.1) | copy-done | bytes 917528
  3.3 0.0 copy-start.2
  3.3 1.0 %copy-done.2 = f32[1792,64]{0,1:T(8,128)S(1)} copy-done((f32[1792,64]{0,1:T(8,128)S(1)}, f32[1792,64]{0,1:T(8,128)}, u32[]{:S(2)}) %copy-start.2) | copy-done | bytes 458776
  4.3 35.2 %reduce.1 = (f32[256,1792]{1,0:T(8,128)S(1)}, f32[112,8,128]{2,1,0:T(8,128)S(1)}, bf16[256,256]{1,0:T(8,128)(2,1)S(1)}, bf16[64,256]{1,0:T(8,128)(2,1)S(1)}, f32[64,256]{1,0:T(8,128)S(1)}) custom-call(bf16[256,1792]{1,0:T(8,128)(2,1)S(1)} %bitcast.7, f32[256,1792]{1,0:T(8,128)S(1)} %bitcast.6, f32[64,1792]{1,0:T(8,128)S(1)} %bitcast.8), custom_call_target="tpu_custom_call" | custom-call | tf_op jit(solution)/shard_map/reduce/pallas_call | solution.py:305
  39.5 2.6 %finish.1 = (f32[256,1792]{1,0:T(8,128)}, f32[64,1792]{1,0:T(8,128)}, f32[64,256]{1,0:T(8,128)}) custom-call(f32[256,1792]{1,0:T(8,128)S(1)} %get-tuple-element.11.m_ref, f32[112,8,128]{2,1,0:T(8,128)S(1)} %get-tuple-element.12.t_ref, bf16[256,256]{1,0:T(8,128)(2,1)S(1)} %get-tuple-element.13.b_ref, bf16[64,256]{1,0:T(8,128)(2,1)S(1)} %get-tuple-element.14.w_ref, ...), custom_call_target="tpu_custom_call" | custom-call | tf_op jit(solution)/shard_map/finish/pallas_call | solution.py:338
Async XLA Ops:
  0.6 1.5 %copy-start = (f32[1,256,1792]{2,1,0:T(8,128)S(1)}, f32[1,256,1792]{2,1,0:T(8,128)}, u32[]{:S(2)}) copy-start(f32[1,256,1792]{2,1,0:T(8,128)} %param.4) | copy-start | bytes 5505028
  2.1 1.2 %copy-start.1 = (bf16[1,256,1792]{2,1,0:T(8,128)(2,1)S(1)}, bf16[1,256,1792]{2,1,0:T(8,128)(2,1)}, u32[]{:S(2)}) copy-start(bf16[1,256,1792]{2,1,0:T(8,128)(2,1)} %param.3) | copy-start | bytes 2752516
  3.3 1.0 %copy-start.2 = (f32[1792,64]{0,1:T(8,128)S(1)}, f32[1792,64]{0,1:T(8,128)}, u32[]{:S(2)}) copy-start(f32[1792,64]{0,1:T(8,128)} %param.5) | copy-start | bytes 1376260

commit v3 on v2

--- a/solution.py
+++ b/solution.py
@@ -43,14 +43,16 @@
 
 def reduce_kernel(
     n, inner, outer, tensor,
-    g_hbm, r_hbm, q_ref, m_ref, t_ref, b_ref, w_ref, basis_ref,
-    g_in, r_in, m_hi, m_lo, left_own, left_in, left_mid, left_all,
-    t_own, t_in, t_sum, t_in2, t_all, gram_b, sems_load, sems_send, sems_recv,
+    g_hbm, r_hbm, q_hbm, m_ref, t_ref, b_ref, w_ref, basis_ref,
+    q_ref, g_in, r_in, m_hi, m_lo, left_own, left_in, left_mid, left_all,
+    t_own, t_in, t_sum, t_in2, t_all, gram_b, sem_q, sems_load, sems_send, sems_recv,
 ):
     rows, cols = g_in.shape
     rank = q_ref.shape[0]
     block = 2 * LANE
     starts = range(0, cols, block)
+    load_q = pltpu.make_async_copy(q_hbm, q_ref, sem_q)
+    load_q.start()
     loads = []
     for j, c in enumerate(starts):
         here = pl.ds(c, block)
@@ -111,6 +113,7 @@
     def landed(dst, slot):
         remote(dst, dst, slot, near_device(1)[1]).wait_recv()
 
+    load_q.wait()
     q_hi, q_lo = split(q_ref[...])
     q_two = jnp.concatenate([q_hi, q_lo], axis=0)
     total = jnp.zeros((2 * rank, rows), jnp.float32)
@@ -311,9 +314,10 @@
             jax.ShapeDtypeStruct((rank, 4 * rank), bf16),
             jax.ShapeDtypeStruct((rank, rows), f32),
         ),
-        in_specs=[hbm, hbm, vmem],
+        in_specs=[hbm] * 3,
         out_specs=(vmem,) * 5,
         scratch_shapes=[
+            pltpu.VMEM((rank, cols), f32),
             pltpu.VMEM((rows, cols), bf16),
             pltpu.VMEM((rows, cols), f32),
             pltpu.VMEM((rows, cols), bf16),
@@ -328,13 +332,14 @@
             tile(outer, small),
             tile(n * small),
             pltpu.VMEM((2 * rank, rows), f32),
+            pltpu.SemaphoreType.DMA,
             pltpu.SemaphoreType.DMA((2, chunks)),
             pltpu.SemaphoreType.DMA((copies,)),
             pltpu.SemaphoreType.DMA((copies,)),
         ],
         compiler_params=pltpu.CompilerParams(collective_id=0, has_side_effects=True, vmem_limit_bytes=VMEM_LIMIT),
         name="reduce",
-    )(grads[0], residual[0], q_prev.T)
+    )(*(pltpu.with_memory_space_constraint(x, pltpu.HBM) for x in (grads[0], residual[0], q_prev.T)))
     new, q_next, basis = pl.pallas_call(
         finish_kernel,
         out_shape=(

time: 42.3 us -> 39.4 us (0.931)
  local copies, waits for them, and re-layouts: 3.69 us -> 0 us
  Pallas kernels: 37.8 us -> 38.6 us
    unnamed x6 -> x0, local copies, waits for them, and re-layouts: 3.69 us -> none
    pallas_call x1, Pallas kernels: 35.2 us -> 36 us  [local(): pl.pallas_call(functools.partial(reduce_kernel, n, inner, outer, tensor),...]
where the time goes in v3:
time: 39.4 us; the launch traced here: 39.2 us
  Pallas kernels  38.6 us (98%)
  between operations  0.64 us (2%)
    pallas_call x1, Pallas kernels, local(): pl.pallas_call(functools.partial(reduce_kernel, n, inner, outer, tensor),...  36 us
    pallas_call x1, Pallas kernels, local(): pl.pallas_call(finish_kernel, out_shape=(jax.ShapeDtypeStruct((rows, cols...  2.58 us

profile of v3, /device:TPU:0, one launch (start us, length us, event | category | flops | bytes accessed | tf_op | source)
XLA Modules:
  0.0 39.2 jit_solution(8395749869027389866)
XLA Ops:
  0.6 36.0 %reduce.1 = (f32[256,1792]{1,0:T(8,128)S(1)}, f32[112,8,128]{2,1,0:T(8,128)S(1)}, bf16[256,256]{1,0:T(8,128)(2,1)S(1)}, bf16[64,256]{1,0:T(8,128)(2,1)S(1)}, f32[64,256]{1,0:T(8,128)S(1)}) custom-call(bf16[256,1792]{1,0:T(8,128)(2,1)} %bitcast.7, f32[256,1792]{1,0:T(8,128)} %bitcast.6, f32[64,1792]{1,0:T(8,128)} %bitcast.8), custom_call_target="tpu_custom_call" | custom-call | tf_op jit(solution)/shard_map/reduce/pallas_call | solution.py:308
  36.7 2.6 %finish.1 = (f32[256,1792]{1,0:T(8,128)}, f32[64,1792]{1,0:T(8,128)}, f32[64,256]{1,0:T(8,128)}) custom-call(f32[256,1792]{1,0:T(8,128)S(1)} %get-tuple-element.11.m_ref, f32[112,8,128]{2,1,0:T(8,128)S(1)} %get-tuple-element.12.t_ref, bf16[256,256]{1,0:T(8,128)(2,1)S(1)} %get-tuple-element.13.b_ref, bf16[64,256]{1,0:T(8,128)(2,1)S(1)} %get-tuple-element.14.w_ref, ...), custom_call_target="tpu_custom_call" | custom-call | tf_op jit(solution)/shard_map/finish/pallas_call | solution.py:343

commit v4 on v3

--- a/solution.py
+++ b/solution.py
@@ -12,6 +12,10 @@
 SUB, LANE = 8, 128
 FIRST_STEPS = 40
 VMEM_LIMIT = 24 << 20
+
+
+def columns_at_once(cols):
+    return cols // 2 if cols % (2 * LANE) == 0 else LANE
 
 
 def split(x):
@@ -49,7 +53,7 @@
 ):
     rows, cols = g_in.shape
     rank = q_ref.shape[0]
-    block = 2 * LANE
+    block = columns_at_once(cols)
     starts = range(0, cols, block)
     load_q = pltpu.make_async_copy(q_hbm, q_ref, sem_q)
     load_q.start()
@@ -266,7 +270,7 @@
 ):
     rank, cols = next_out.shape
     tall = rank // SUB
-    block = 2 * LANE
+    block = columns_at_once(cols)
     out_basis_ref[...] = basis_ref[...]
     stores = []
     for j, c in enumerate(range(0, cols, block)):
@@ -304,7 +308,7 @@
     tile = lambda *dims: pltpu.VMEM((*dims, SUB, LANE), f32)
     vmem = pl.BlockSpec(memory_space=pltpu.VMEM)
     hbm = pl.BlockSpec(memory_space=pltpu.HBM)
-    chunks = cols // (2 * LANE)
+    chunks = cols // columns_at_once(cols)
     merged, t_sum, b_four, w_four, basis = pl.pallas_call(
         functools.partial(reduce_kernel, n, inner, outer, tensor),
         out_shape=(

time: 39.4 us -> 38.9 us (0.987)
  Pallas kernels: 38.6 us -> 38.1 us
where the time goes in v4:
time: 38.9 us; the launch traced here: 38.7 us
  Pallas kernels  38.1 us (98%)
  between operations  0.64 us (2%)
    pallas_call x1, Pallas kernels, local(): pl.pallas_call(functools.partial(reduce_kernel, n, inner, outer, tensor),...  35.7 us
    pallas_call x1, Pallas kernels, local(): pl.pallas_call(finish_kernel, out_shape=(jax.ShapeDtypeStruct((rows, cols...  2.44 us

profile of v4, /device:TPU:0, one launch (start us, length us, event | category | flops | bytes accessed | tf_op | source)
XLA Modules:
  0.0 38.7 jit_solution(14475034057275502355)
XLA Ops:
  0.6 35.7 %reduce.1 = (f32[256,1792]{1,0:T(8,128)S(1)}, f32[112,8,128]{2,1,0:T(8,128)S(1)}, bf16[256,256]{1,0:T(8,128)(2,1)S(1)}, bf16[64,256]{1,0:T(8,128)(2,1)S(1)}, f32[64,256]{1,0:T(8,128)S(1)}) custom-call(bf16[256,1792]{1,0:T(8,128)(2,1)} %bitcast.7, f32[256,1792]{1,0:T(8,128)} %bitcast.6, f32[64,1792]{1,0:T(8,128)} %bitcast.8), custom_call_target="tpu_custom_call" | custom-call | tf_op jit(solution)/shard_map/reduce/pallas_call | solution.py:312
  36.3 2.4 %finish.1 = (f32[256,1792]{1,0:T(8,128)}, f32[64,1792]{1,0:T(8,128)}, f32[64,256]{1,0:T(8,128)}) custom-call(f32[256,1792]{1,0:T(8,128)S(1)} %get-tuple-element.11.m_ref, f32[112,8,128]{2,1,0:T(8,128)S(1)} %get-tuple-element.12.t_ref, bf16[256,256]{1,0:T(8,128)(2,1)S(1)} %get-tuple-element.13.b_ref, bf16[64,256]{1,0:T(8,128)(2,1)S(1)} %get-tuple-element.14.w_ref, ...), custom_call_target="tpu_custom_call" | custom-call | tf_op jit(solution)/shard_map/finish/pallas_call | solution.py:347
